TPU v7x, 128 devices: a whole 4x4x4 slice. The times are simulated.
128 devices in a mesh: seq: 16 (over z, y_hi, core), chan: 8 (over y_lo, x).
Axes of the slice: x: 4, y: 4 (y_hi: 2, y_lo: 2; y = y_hi * 2 + y_lo), z: 4, core: 2. Of those that a mesh axis runs over, the one named last changes fastest.
Arguments:
- values: bfloat16 [4096, 4096], P('seq', 'chan'), may hold values from -6 to 6
- gates: bfloat16 [4096, 4096], P('seq', 'chan'), may hold values from -6 to 6
- filters: bfloat16 [1024, 4096], P(None, 'chan'), may hold values from -2 to 2
- skip: float32 [4096], P('chan'), may hold values from -4 to 4
- out_weight: bfloat16 [4096, 4096], P(('seq', 'chan')), may hold values from -0.09375 to 0.09375
Outputs:
- projected: bfloat16 [4096, 4096], P(('seq', 'chan'))
All inputs are finite; a program needn't handle non-finite values.
Results may differ from a plain program's by a relative error of at most 0.009.
Values may be sent and summed in bfloat16 or wider, within the bound.
A program may use at most 128 MiB of HBM per device.

v0:
```python
import numpy as np
import jax
import jax.numpy as jnp
from jax import lax
from jax.sharding import PartitionSpec as P


def dft_tables(block):
    size = 2 * block
    freq = (np.arange(block) + 0.5)[:, None]
    angle = 2.0 * np.pi * freq * np.arange(size)[None, :] / size
    forward = np.concatenate([np.cos(angle), -np.sin(angle)], axis=0)
    late = angle[:, block:]
    backward = np.concatenate([np.cos(late), -np.sin(late)], axis=0).T / block
    return (forward, backward)


def from_behind(value, axis, steps):
    count = lax.axis_size(axis)
    return lax.ppermute(value, axis, [(source, source + steps) for source in range(count - steps)])


def dot(a, b):
    return jnp.dot(a, b, preferred_element_type=jnp.float32)


def body(values, gates, filters, skip, out_weight):
    block = values.shape[0]
    taps = filters.shape[0] // block
    forward, backward = dft_tables(block)
    forward = jnp.asarray(forward, jnp.bfloat16)
    backward = jnp.asarray(backward, jnp.bfloat16)
    part = lax.all_to_all(out_weight, "chan", split_axis=1, concat_axis=0, tiled=True)
    columns = lax.all_gather(part, "seq", axis=0, tiled=True)
    blocks = [values] + [from_behind(values, "seq", step) for step in range(1, taps + 1)]
    real = 0.0
    imag = 0.0
    for j in range(taps):
        kernel = dot(forward[:, :block], filters[j * block : (j + 1) * block])
        window = dot(forward, jnp.concatenate([blocks[j + 1], blocks[j]], axis=0))
        kr, ki = (kernel[:block], kernel[block:])
        wr, wi = (window[:block], window[block:])
        real = real + kr * wr - ki * wi
        imag = imag + kr * wi + ki * wr
    spectrum = jnp.concatenate([real, imag], axis=0).astype(jnp.bfloat16)
    filtered = dot(backward, spectrum) + skip[None, :] * values.astype(jnp.float32)
    gated = (gates.astype(jnp.float32) * filtered).astype(jnp.bfloat16)
    rows = lax.all_gather(gated, "chan", axis=1, tiled=True)
    summed = dot(rows, columns).astype(jnp.bfloat16)
    return lax.all_to_all(summed, "chan", split_axis=0, concat_axis=1, tiled=True)


def solution(mesh):
    in_specs = (
        P("seq", "chan"),
        P("seq", "chan"),
        P(None, "chan"),
        P("chan"),
        P(("seq", "chan"), None),
    )
    out_specs = P(("seq", "chan"), None)
    return jax.shard_map(body, mesh=mesh, in_specs=in_specs, out_specs=out_specs, check_vma=False)
```

profile of v0, /device:TPU:1, one launch (start us, length us, event | category | flops | bytes accessed | tf_op | source)
XLA Modules:
  0.0 166.8 jit_solution(8608560338992499461)
XLA Ops:
  6.5 0.0 all-gather.3.cloned.1.call-start
  6.5 6.5 %collective-permute-start.1 = (bf16[256,512]{1,0:T(8,128)(2,1)}, bf16[256,512]{1,0:T(8,128)(2,1)}, u32[]{:S(2)}, u32[]{:S(2)}) collective-permute-start(bf16[256,512]{1,0:T(8,128)(2,1)} %param.7), channel_id=1, source_target_pairs={{0,16},{8,24},{16,32},{24,40},{32,48},{40,56},{48,64},{56,72},{64,... | collective-permute-start | bytes 786440 | tf_op jit(solution)/shard_map/ppermute | solution.py:20
  13.0 4.4 %collective-permute-start.2 = (bf16[256,512]{1,0:T(8,128)(2,1)}, bf16[256,512]{1,0:T(8,128)(2,1)}, u32[]{:S(2)}, u32[]{:S(2)}) collective-permute-start(bf16[256,512]{1,0:T(8,128)(2,1)} %param.7), channel_id=1, source_target_pairs={{0,24},{8,32},{16,40},{24,48},{32,56},{40,64},{48,72},{56,80},{64,... | collective-permute-start | bytes 786440 | tf_op jit(solution)/shard_map/ppermute | solution.py:20
  17.4 4.0 %collective-permute-start = (bf16[256,512]{1,0:T(8,128)(2,1)}, bf16[256,512]{1,0:T(8,128)(2,1)}, u32[]{:S(2)}, u32[]{:S(2)}) collective-permute-start(bf16[256,512]{1,0:T(8,128)(2,1)} %param.7), channel_id=1, source_target_pairs={{0,8},{8,16},{16,24},{24,32},{32,40},{40,48},{48,56},{56,64},{64,7... | collective-permute-start | bytes 786440 | tf_op jit(solution)/shard_map/ppermute | solution.py:20
  21.4 3.6 %collective-permute-start.3 = (bf16[256,512]{1,0:T(8,128)(2,1)}, bf16[256,512]{1,0:T(8,128)(2,1)}, u32[]{:S(2)}, u32[]{:S(2)}) collective-permute-start(bf16[256,512]{1,0:T(8,128)(2,1)} %param.7), channel_id=1, source_target_pairs={{0,32},{8,40},{16,48},{24,56},{32,64},{40,72},{48,80},{56,88},{64,... | collective-permute-start | bytes 786440 | tf_op jit(solution)/shard_map/ppermute | solution.py:20
  25.0 1.3 fusion.10
  26.3 1.3 fusion.4
  27.6 1.3 fusion.6
  29.0 0.0 copy-done
  29.0 2.2 %fusion.8 = f32[512,512]{1,0:T(8,128)} fusion(bf16[512,256]{1,0:T(8,128)(2,1)S(1)} %copy-done, bf16[1024,512]{1,0:T(8,128)(2,1)} %param.9), kind=kOutput, calls=%fused_computation.17 | convolution fusion | flops 134217728 | bytes 1572864 | tf_op jit(solution)/shard_map/dot_general | solution.py:24
  31.2 1.8 %copy.15 = bf16[256,512]{0,1:T(8,128)(2,1)} copy(bf16[256,512]{1,0:T(8,128)(2,1)} %param.7) | data formatting | bytes 524288 | tf_op args[0]
  33.0 1.8 %copy.14 = bf16[256,512]{0,1:T(8,128)(2,1)} copy(bf16[256,512]{1,0:T(8,128)(2,1)} %param.8) | data formatting | bytes 524288 | tf_op args[1]
  34.8 1.4 fusion.13
  36.2 0.0 collective-permute-done
  36.2 1.2 convolution_add_fusion.3
  37.4 0.0 copy-done.2
  37.4 1.2 fusion.14
  38.7 0.0 collective-permute-done.1
  38.7 1.2 convolution_add_fusion.2
  39.9 0.0 copy-start.1
  39.9 0.0 copy-start.7
  40.0 1.3 fusion.15
  41.3 0.0 collective-permute-done.2
  41.3 1.2 convolution_add_fusion.1
  42.6 0.0 copy-start.3
  42.6 0.0 copy-start.4
  42.6 0.0 copy-start.6
  42.6 0.0 copy-start.8
  42.6 1.3 fusion.16
  43.9 0.0 collective-permute-done.3
  43.9 1.2 convolution_add_fusion
  45.2 0.0 copy-done.1
  45.2 0.0 copy-start.5
  45.2 1.0 fusion.12
  46.2 0.0 copy-done.3
  46.2 0.0 copy-done.4
  46.2 0.0 copy-done.6
  46.2 0.0 copy-done.8
  46.2 1.7 %fusion.3 = bf16[256,512]{0,1:T(8,128)(2,1)} fusion(f32[512,256]{1,0:T(8,128)S(1)} %fusion.12, bf16[256,256]{1,0:T(8,128)(2,1)S(1)} %copy-done.6, bf16[256,512]{0,1:T(8,128)(2,1)S(1)} %copy-done.3, bf16[256,512]{0,1:T(8,128)(2,1)S(1)} %copy-done.4, f32[512]{0:T(512)S(1)} %copy-done.8, f32[512,512]{1,0:T(8,128)S(1)} %convolution_add_fusion, ...), kind=kOutput, calls=%fused_computation.8 | convolution fusion | flops 70123520 | bytes 9832448 | tf_op jit(solution)/shard_map/dot_general | solution.py:24
  47.9 0.0 all-gather.3.cloned.1.call-update
  48.0 0.0 all-gather.5.cloned.1.call-start
  48.0 12.4 %all_to_all.38 = bf16[32,8,512]{2,0,1:T(8,128)(2,1)} all-to-all(bf16[32,8,512]{2,0,1:T(8,128)(2,1)S(1)} %bitcast.45), channel_id=1, replica_groups=mesh['seq'=16,'chan'=8] {'chan'}, dimensions={1} | all-to-all | bytes 524288 | tf_op jit(solution)/shard_map/all_to_all | solution.py:33
  60.4 0.0 all-gather.5.cloned.1.call-update
  60.5 22.0 %all-gather.3.cloned.1.call-done = bf16[256,4096]{0,1:T(8,128)(2,1)} async-done(((bf16[256,512]{0,1:T(8,128)(2,1)}), bf16[256,4096]{0,1:T(8,128)(2,1)}) %all-gather.3.cloned.1.call-update) | async-done | bytes 2097168 | tf_op jit(solution)/shard_map/all_gather | solution.py:48
  82.5 61.5 %all-gather.5.cloned.1.call-done = bf16[4096,512]{1,0:T(8,128)(2,1)} async-done(((bf16[256,512]{1,0:T(8,128)(2,1)}), bf16[4096,512]{1,0:T(8,128)(2,1)}) %all-gather.5.cloned.1.call-update) | async-done | bytes 4194320 | tf_op jit(solution)/shard_map/all_gather | solution.py:34
  144.0 4.1 %convolution_convert_fusion = bf16[256,512]{1,0:T(8,128)(2,1)S(1)} fusion(bf16[256,4096]{0,1:T(8,128)(2,1)} %all-gather.3.cloned.1.call-done, bf16[4096,512]{1,0:T(8,128)(2,1)} %all-gather.5.cloned.1.call-done), kind=kOutput, calls=%fused_computation.9 | convolution fusion | flops 1073872896 | bytes 6553600 | tf_op jit(solution)/shard_map/dot_general | solution.py:24
  148.0 11.2 %all_to_all.39 = bf16[8,32,512]{2,1,0:T(8,128)(2,1)S(1)} all-to-all(bf16[8,32,512]{2,1,0:T(8,128)(2,1)S(1)} %bitcast.47), channel_id=1, replica_groups=mesh['seq'=16,'chan'=8] {'chan'}, dimensions={0} | all-to-all | bytes 524288 | tf_op jit(solution)/shard_map/all_to_all | solution.py:50
  159.3 0.7 copy.19
  (5 shorter events, 0.0 us)
Async XLA Ops:
  6.5 22.4 %copy-start = (bf16[512,256]{1,0:T(8,128)(2,1)S(1)}, bf16[512,256]{1,0:T(8,128)(2,1)}, u32[]{:S(2)}) copy-start(bf16[512,256]{1,0:T(8,128)(2,1)} %constant.7) | copy-start | bytes 786436
  6.5 75.9 %all-gather.3.cloned.1.call-start = ((), (), s32[]{:S(2)}) async-start(), calls=%async_computation.2 | async-start | bytes 2359296 | tf_op jit(solution)/shard_map/all_gather | solution.py:48
  6.5 32.1 %collective-permute-start.1 = (bf16[256,512]{1,0:T(8,128)(2,1)}, bf16[256,512]{1,0:T(8,128)(2,1)}, u32[]{:S(2)}, u32[]{:S(2)}) collective-permute-start(bf16[256,512]{1,0:T(8,128)(2,1)} %param.7), channel_id=1, source_target_pairs={{0,16},{8,24},{16,32},{24,40},{32,48},{40,56},{48,64},{56,72},{64,... | collective-permute-start | bytes 786440 | tf_op jit(solution)/shard_map/ppermute | solution.py:20
  13.0 28.3 %collective-permute-start.2 = (bf16[256,512]{1,0:T(8,128)(2,1)}, bf16[256,512]{1,0:T(8,128)(2,1)}, u32[]{:S(2)}, u32[]{:S(2)}) collective-permute-start(bf16[256,512]{1,0:T(8,128)(2,1)} %param.7), channel_id=1, source_target_pairs={{0,24},{8,32},{16,40},{24,48},{32,56},{40,64},{48,72},{56,80},{64,... | collective-permute-start | bytes 786440 | tf_op jit(solution)/shard_map/ppermute | solution.py:20
  17.4 18.8 %collective-permute-start = (bf16[256,512]{1,0:T(8,128)(2,1)}, bf16[256,512]{1,0:T(8,128)(2,1)}, u32[]{:S(2)}, u32[]{:S(2)}) collective-permute-start(bf16[256,512]{1,0:T(8,128)(2,1)} %param.7), channel_id=1, source_target_pairs={{0,8},{8,16},{16,24},{24,32},{32,40},{40,48},{48,56},{56,64},{64,7... | collective-permute-start | bytes 786440 | tf_op jit(solution)/shard_map/ppermute | solution.py:20
  21.4 22.5 %collective-permute-start.3 = (bf16[256,512]{1,0:T(8,128)(2,1)}, bf16[256,512]{1,0:T(8,128)(2,1)}, u32[]{:S(2)}, u32[]{:S(2)}) collective-permute-start(bf16[256,512]{1,0:T(8,128)(2,1)} %param.7), channel_id=1, source_target_pairs={{0,32},{8,40},{16,48},{24,56},{32,64},{40,72},{48,80},{56,88},{64,... | collective-permute-start | bytes 786440 | tf_op jit(solution)/shard_map/ppermute | solution.py:20
  34.8 2.6 %copy-start.2 = (bf16[512,256]{1,0:T(8,128)(2,1)S(1)}, bf16[512,256]{1,0:T(8,128)(2,1)}, u32[]{:S(2)}) copy-start(bf16[512,256]{1,0:T(8,128)(2,1)} %constant.8) | copy-start | bytes 786436
  39.9 5.2 %copy-start.1 = (f32[512,512]{1,0:T(8,128)S(1)}, f32[512,512]{1,0:T(8,128)}, u32[]{:S(2)}) copy-start(f32[512,512]{1,0:T(8,128)} %fusion.8) | copy-start | bytes 3145732
  39.9 5.2 %copy-start.7 = (bf16[256,256]{1,0:T(8,128)(2,1)S(1)}, bf16[256,256]{1,0:T(8,128)(2,1)}, u32[]{:S(2)}) copy-start(bf16[256,256]{1,0:T(8,128)(2,1)} %constant.9) | copy-start | bytes 393220
  42.6 3.6 %copy-start.3 = (bf16[256,512]{0,1:T(8,128)(2,1)S(1)}, bf16[256,512]{0,1:T(8,128)(2,1)}, u32[]{:S(2)}) copy-start(bf16[256,512]{0,1:T(8,128)(2,1)} %copy.15) | copy-start | bytes 786436
  42.6 3.6 %copy-start.4 = (bf16[256,512]{0,1:T(8,128)(2,1)S(1)}, bf16[256,512]{0,1:T(8,128)(2,1)}, u32[]{:S(2)}) copy-start(bf16[256,512]{0,1:T(8,128)(2,1)} %copy.14) | copy-start | bytes 786436
  42.6 3.6 %copy-start.6 = (bf16[256,256]{1,0:T(8,128)(2,1)S(1)}, bf16[256,256]{1,0:T(8,128)(2,1)}, u32[]{:S(2)}) copy-start(bf16[256,256]{1,0:T(8,128)(2,1)} %constant.10) | copy-start | bytes 393220
  42.6 3.6 %copy-start.8 = (f32[512]{0:T(512)S(1)}, f32[512]{0:T(512)}, u32[]{:S(2)}) copy-start(f32[512]{0:T(512)} %param.10) | copy-start | bytes 6148
  45.2 2.8 %copy-start.5 = (bf16[32,4096]{1,0:T(8,128)(2,1)S(1)}, bf16[32,4096]{1,0:T(8,128)(2,1)}, u32[]{:S(2)}) copy-start(bf16[32,4096]{1,0:T(8,128)(2,1)} %param.11) | copy-start | bytes 786436
  48.0 96.0 %all-gather.5.cloned.1.call-start = ((), (), s32[]{:S(2)}) async-start(), calls=%async_computation.3 | async-start | bytes 4456448 | tf_op jit(solution)/shard_map/all_gather | solution.py:34
Sparse Core Ops, SparseCore 0:
  48.1 34.3 all-gather.2
  84.9 58.9 all-gather.4
where the time goes:
time: 167 us
  waiting for transfers between devices  83.5 us (50%)
  blocking collectives  23.6 us (14%)
  matrix products  23.1 us (14%)
  starting transfers between devices  18.5 us (11%)
  between operations  13.6 us (8%)
  local copies, waits for them, and re-layouts  4.39 us (3%)
    all_gather x1, waiting for transfers between devices, body(): columns = lax.all_gather(part, 'seq', axis=0, tiled=True)  61.5 us
    dot_general x15, matrix products, dot(): return jnp.dot(a, b, preferred_element_type=jnp.float32)  23.1 us
    all_gather x1, waiting for transfers between devices, body(): rows = lax.all_gather(gated, 'chan', axis=1, tiled=True)  22 us
    ppermute x4, starting transfers between devices, from_behind(): lax.ppermute(value, axis, [(source, source + steps) for source in range(c...  18.5 us
    all_to_all x1, blocking collectives, body(): lax.all_to_all(out_weight, 'chan', split_axis=1, concat_axis=0, tiled=True)  12.4 us
    all_to_all x1, blocking collectives, body(): lax.all_to_all(summed, 'chan', split_axis=0, concat_axis=1, tiled=True)  11.2 us
    unnamed x20, local copies, waits for them, and re-layouts  3.65 us
  transfers between devices with their start and end apart: 6, of which 2 were waited for; matrix products, arithmetic and copies ran while one was open for 11% of the time, Pallas kernels for 0%

commit v1 on v0

--- a/solution.py
+++ b/solution.py
@@ -45,7 +45,9 @@
     spectrum = jnp.concatenate([real, imag], axis=0).astype(jnp.bfloat16)
     filtered = dot(backward, spectrum) + skip[None, :] * values.astype(jnp.float32)
     gated = (gates.astype(jnp.float32) * filtered).astype(jnp.bfloat16)
-    rows = lax.all_gather(gated, "chan", axis=1, tiled=True)
+    rows = jnp.concatenate(
+        lax.all_to_all(jnp.stack([gated] * lax.axis_size("chan")), "chan", 0, 0), axis=1
+    )
     summed = dot(rows, columns).astype(jnp.bfloat16)
     return lax.all_to_all(summed, "chan", split_axis=0, concat_axis=1, tiled=True)
 

time: 167 us -> 122 us (0.73)
  the two profiles are of different devices: /device:TPU:1 before, /device:TPU:16 now
where the time goes in v1:
time: 122 us; the launch traced here: 121 us
  blocking collectives  57 us (47%)
  waiting for transfers between devices  24.5 us (20%)
  between operations  13.6 us (11%)
  starting transfers between devices  13.3 us (11%)
  matrix products  8.48 us (7%)
  local copies, waits for them, and re-layouts  4.42 us (4%)
    all_to_all x1, blocking collectives, body(): lax.all_to_all(jnp.stack([gated] * lax.axis_size('chan')), 'chan', 0, 0)  31.5 us
    all_gather x1, waiting for transfers between devices, body(): columns = lax.all_gather(part, 'seq', axis=0, tiled=True)  21.2 us
    ppermute x4, starting transfers between devices, from_behind(): lax.ppermute(value, axis, [(source, source + steps) for source in range(c...  13.3 us
    all_to_all x1, blocking collectives, body(): lax.all_to_all(summed, 'chan', split_axis=0, concat_axis=1, tiled=True)  13.3 us
    all_to_all x1, blocking collectives, body(): lax.all_to_all(out_weight, 'chan', split_axis=1, concat_axis=0, tiled=True)  12.2 us
    dot_general x15, matrix products, dot(): return jnp.dot(a, b, preferred_element_type=jnp.float32)  8.48 us
    ppermute x4, waiting for transfers between devices, from_behind(): lax.ppermute(value, axis, [(source, source + steps) for source in range(c...  3.28 us
    unnamed x16, local copies, waits for them, and re-layouts  2.49 us
  transfers between devices with their start and end apart: 5, of which 3 were waited for; matrix products, arithmetic and copies ran while one was open for 6% of the time, Pallas kernels for 0%

profile of v1, /device:TPU:16, one launch (start us, length us, event | category | flops | bytes accessed | tf_op | source)
XLA Modules:
  0.0 121.3 jit_solution(3758610942815144316)
XLA Ops:
  6.5 0.0 copy-start
  6.5 0.0 copy-start.3
  6.5 0.0 all-gather.2.cloned.1.call-start
  6.5 1.1 copy.26
  7.6 12.2 %all_to_all.43 = bf16[32,8,512]{2,0,1:T(8,128)(2,1)} all-to-all(bf16[32,8,512]{2,0,1:T(8,128)(2,1)S(1)} %bitcast.49), channel_id=1, replica_groups=mesh['seq'=16,'chan'=8] {'chan'}, dimensions={1} | all-to-all | bytes 524288 | tf_op jit(solution)/shard_map/all_to_all | solution.py:33
  19.8 0.0 all-gather.2.cloned.1.call-update
  19.8 3.9 %collective-permute-start.1 = (bf16[256,512]{1,0:T(8,128)(2,1)}, bf16[256,512]{1,0:T(8,128)(2,1)S(1)}, u32[]{:S(2)}, u32[]{:S(2)}) collective-permute-start(bf16[256,512]{1,0:T(8,128)(2,1)} %param.7), channel_id=1, source_target_pairs={{0,16},{8,24},{16,32},{24,40},{32,48},{40,56},{48,64},{56,72},{64,... | collective-permute-start | bytes 786440 | tf_op jit(solution)/shard_map/ppermute | solution.py:20
  23.8 2.7 %collective-permute-start.2 = (bf16[256,512]{1,0:T(8,128)(2,1)}, bf16[256,512]{1,0:T(8,128)(2,1)S(1)}, u32[]{:S(2)}, u32[]{:S(2)}) collective-permute-start(bf16[256,512]{1,0:T(8,128)(2,1)} %param.7), channel_id=1, source_target_pairs={{0,24},{8,32},{16,40},{24,48},{32,56},{40,64},{48,72},{56,80},{64,... | collective-permute-start | bytes 786440 | tf_op jit(solution)/shard_map/ppermute | solution.py:20
  26.5 3.1 %collective-permute-start = (bf16[256,512]{1,0:T(8,128)(2,1)}, bf16[256,512]{1,0:T(8,128)(2,1)S(1)}, u32[]{:S(2)}, u32[]{:S(2)}) collective-permute-start(bf16[256,512]{1,0:T(8,128)(2,1)} %param.7), channel_id=1, source_target_pairs={{0,8},{8,16},{16,24},{24,32},{32,40},{40,48},{48,56},{56,64},{64,7... | collective-permute-start | bytes 786440 | tf_op jit(solution)/shard_map/ppermute | solution.py:20
  29.6 3.5 %collective-permute-start.3 = (bf16[256,512]{1,0:T(8,128)(2,1)}, bf16[256,512]{1,0:T(8,128)(2,1)S(1)}, u32[]{:S(2)}, u32[]{:S(2)}) collective-permute-start(bf16[256,512]{1,0:T(8,128)(2,1)} %param.7), channel_id=1, source_target_pairs={{0,32},{8,40},{16,48},{24,56},{32,64},{40,72},{48,80},{56,88},{64,... | collective-permute-start | bytes 786440 | tf_op jit(solution)/shard_map/ppermute | solution.py:20
  33.2 1.1 copy.20
  34.3 1.1 copy.19
  35.4 0.0 copy-done
  35.4 0.0 copy-done.3
  35.4 0.3 fusion.10
  35.7 0.0 copy-start.1
  35.7 0.0 copy-start.2
  35.7 0.3 fusion.4
  36.0 0.3 fusion.6
  36.3 0.3 fusion.8
  36.6 0.0 copy-done.1
  36.7 0.1 copy-done.2
  36.7 0.3 fusion.13
  37.0 1.6 %collective-permute-done = bf16[256,512]{1,0:T(8,128)(2,1)S(1)} collective-permute-done((bf16[256,512]{1,0:T(8,128)(2,1)}, bf16[256,512]{1,0:T(8,128)(2,1)S(1)}, u32[]{:S(2)}, u32[]{:S(2)}) %collective-permute-start) | collective-permute-done | bytes 262176 | tf_op jit(solution)/shard_map/ppermute | solution.py:20
  38.7 0.3 convolution_add_fusion.3
  39.0 0.3 fusion.14
  39.2 0.0 collective-permute-done.1
  39.3 0.3 convolution_add_fusion.2
  39.6 0.3 fusion.15
  39.8 0.0 collective-permute-done.2
  39.9 0.3 convolution_add_fusion.1
  40.2 0.0 copy-start.5
  40.2 0.3 fusion.16
  40.5 1.6 %collective-permute-done.3 = bf16[256,512]{1,0:T(8,128)(2,1)S(1)} collective-permute-done((bf16[256,512]{1,0:T(8,128)(2,1)}, bf16[256,512]{1,0:T(8,128)(2,1)S(1)}, u32[]{:S(2)}, u32[]{:S(2)}) %collective-permute-start.3) | collective-permute-done | bytes 262176 | tf_op jit(solution)/shard_map/ppermute | solution.py:20
  42.1 0.3 convolution_add_fusion
  42.4 0.0 copy-done.5
  42.4 0.0 copy-start.4
  42.4 0.0 copy-start.6
  42.4 0.8 fusion.12
  43.2 0.1 copy-done.4
  43.3 0.0 copy-done.6
  43.3 0.8 fusion.3
  44.1 0.1 stack.2
  44.3 31.5 %all_to_all.44 = bf16[8,256,512]{1,2,0:T(8,128)(2,1)S(1)} all-to-all(bf16[8,256,512]{1,2,0:T(8,128)(2,1)S(1)} %stack.2), channel_id=1, replica_groups=mesh['seq'=16,'chan'=8] {'chan'}, dimensions={0} | all-to-all | bytes 4194304 | tf_op jit(solution)/shard_map/all_to_all | solution.py:49
  75.8 21.2 %all-gather.2.cloned.1.call-done = bf16[4096,512]{1,0:T(8,128)(2,1)} async-done(((bf16[256,512]{1,0:T(8,128)(2,1)}), bf16[4096,512]{1,0:T(8,128)(2,1)}) %all-gather.2.cloned.1.call-update) | async-done | bytes 4194320 | tf_op jit(solution)/shard_map/all_gather | solution.py:34
  97.0 3.4 %convolution_convert_fusion = bf16[256,512]{1,0:T(8,128)(2,1)S(1)} fusion(bf16[256,4096]{0,1:T(8,128)(2,1)S(1)} %bitcast.46, bf16[4096,512]{1,0:T(8,128)(2,1)} %all-gather.2.cloned.1.call-done), kind=kOutput, calls=%fused_computation.9 | convolution fusion | flops 1073872896 | bytes 6553600 | tf_op jit(solution)/shard_map/dot_general | solution.py:24
  100.5 13.3 %all_to_all.45 = bf16[8,32,512]{2,1,0:T(8,128)(2,1)S(1)} all-to-all(bf16[8,32,512]{2,1,0:T(8,128)(2,1)S(1)} %bitcast.51), channel_id=1, replica_groups=mesh['seq'=16,'chan'=8] {'chan'}, dimensions={0} | all-to-all | bytes 524288 | tf_op jit(solution)/shard_map/all_to_all | solution.py:52
  113.8 0.7 copy.24
Async XLA Ops:
  6.5 28.9 %copy-start = (bf16[512,256]{1,0:T(8,128)(2,1)S(1)}, bf16[512,256]{1,0:T(8,128)(2,1)}, u32[]{:S(2)}) copy-start(bf16[512,256]{1,0:T(8,128)(2,1)} %constant.7) | copy-start | bytes 786436
  6.5 28.9 %copy-start.3 = (bf16[1024,512]{1,0:T(8,128)(2,1)S(1)}, bf16[1024,512]{1,0:T(8,128)(2,1)}, u32[]{:S(2)}) copy-start(bf16[1024,512]{1,0:T(8,128)(2,1)} %param.9) | copy-start | bytes 3145732
  6.5 90.5 %all-gather.2.cloned.1.call-start = ((), (), s32[]{:S(2)}) async-start(), calls=%async_computation.3 | async-start | bytes 4456448 | tf_op jit(solution)/shard_map/all_gather | solution.py:34
  19.8 19.4 %collective-permute-start.1 = (bf16[256,512]{1,0:T(8,128)(2,1)}, bf16[256,512]{1,0:T(8,128)(2,1)S(1)}, u32[]{:S(2)}, u32[]{:S(2)}) collective-permute-start(bf16[256,512]{1,0:T(8,128)(2,1)} %param.7), channel_id=1, source_target_pairs={{0,16},{8,24},{16,32},{24,40},{32,48},{40,56},{48,64},{56,72},{64,... | collective-permute-start | bytes 786440 | tf_op jit(solution)/shard_map/ppermute | solution.py:20
  23.8 16.1 %collective-permute-start.2 = (bf16[256,512]{1,0:T(8,128)(2,1)}, bf16[256,512]{1,0:T(8,128)(2,1)S(1)}, u32[]{:S(2)}, u32[]{:S(2)}) collective-permute-start(bf16[256,512]{1,0:T(8,128)(2,1)} %param.7), channel_id=1, source_target_pairs={{0,24},{8,32},{16,40},{24,48},{32,56},{40,64},{48,72},{56,80},{64,... | collective-permute-start | bytes 786440 | tf_op jit(solution)/shard_map/ppermute | solution.py:20
  26.5 12.2 %collective-permute-start = (bf16[256,512]{1,0:T(8,128)(2,1)}, bf16[256,512]{1,0:T(8,128)(2,1)S(1)}, u32[]{:S(2)}, u32[]{:S(2)}) collective-permute-start(bf16[256,512]{1,0:T(8,128)(2,1)} %param.7), channel_id=1, source_target_pairs={{0,8},{8,16},{16,24},{24,32},{32,40},{40,48},{48,56},{56,64},{64,7... | collective-permute-start | bytes 786440 | tf_op jit(solution)/shard_map/ppermute | solution.py:20
  29.6 12.5 %collective-permute-start.3 = (bf16[256,512]{1,0:T(8,128)(2,1)}, bf16[256,512]{1,0:T(8,128)(2,1)S(1)}, u32[]{:S(2)}, u32[]{:S(2)}) collective-permute-start(bf16[256,512]{1,0:T(8,128)(2,1)} %param.7), channel_id=1, source_target_pairs={{0,32},{8,40},{16,48},{24,56},{32,64},{40,72},{48,80},{56,88},{64,... | collective-permute-start | bytes 786440 | tf_op jit(solution)/shard_map/ppermute | solution.py:20
  35.7 1.0 copy-start.1
  35.7 1.0 copy-start.2
  40.2 2.2 %copy-start.5 = (bf16[256,256]{1,0:T(8,128)(2,1)S(1)}, bf16[256,256]{1,0:T(8,128)(2,1)}, u32[]{:S(2)}) copy-start(bf16[256,256]{1,0:T(8,128)(2,1)} %constant.9) | copy-start | bytes 393220
  42.4 0.9 copy-start.4
  42.4 0.9 copy-start.6
Sparse Core Ops, SparseCore 0:
  20.0 77.0 all-gather.1
